TPU v7x, 128 devices: a whole 4x4x4 slice. The times are simulated.
128 devices in a mesh: gz: 16 (over z_hi, x, core), xy: 8 (over z_lo, y).
Axes of the slice: x: 4, y: 4, z: 4 (z_hi: 2, z_lo: 2; z = z_hi * 2 + z_lo), core: 2. Of those that a mesh axis runs over, the one named last changes fastest.
Arguments:
- prior_estimate: float32 [768, 256, 128], P('gz', 'xy'), may hold values from 0.5 to 2
- views_upright: float32 [3, 768, 256, 128], P(None, 'gz', 'xy'), may hold values from 0.2 to 5
- views_turned: float32 [3, 768, 128, 256], P(None, 'gz', 'xy'), may hold values from 0.2 to 5
- kernel_depth: float32 [6, 61], replicated, may hold values from 0.005 to 1.55, as said below
- kernel_rows: float32 [6, 31], replicated, may hold values from 0.005 to 1.55, as said below
- kernel_columns: float32 [6, 31], replicated, may hold values from 0.005 to 1.55, as said below
- lateral_offsets: int32 [6], replicated, may hold values from -8 to 8, as said below
- block_views: int32 [128, 3], replicated, may hold values from 0 to 5, all different within a row
Outputs:
- estimate: float32 [768, 256, 128], P('gz', 'xy')
Inputs may be any that keep to these rules, and one draw needn't show every extreme that they name: `block_views`: row r holds 3 different views and belongs to the block at position r // 8 along gz and r % 8 along xy. `lateral_offsets`: one view has offset 8 and another -8. `kernel_depth`: positive taps. `kernel_rows`: positive taps. `kernel_columns`: positive taps.
All inputs are finite; a program needn't handle non-finite values.
Results may differ from a plain program's by a relative error of at most 0.00005.
Values sent between devices are 32-bit elements; how exact they have to be, the bound alone decides.
A program may use at most 128 MiB of HBM per device.

v0:
```python
import jax
import jax.numpy as jnp
from jax import lax
from jax.sharding import PartitionSpec as P

ITERS = 2
exact_mode = lax.Precision.HIGHEST


def padded(cells, sides, width):
    for axis, dim in sides:
        count = lax.axis_size(axis)
        ends = count - 1
        head = lax.slice_in_dim(cells, 0, width, axis=dim)
        tail = lax.slice_in_dim(cells, cells.shape[dim] - width, cells.shape[dim], axis=dim)
        cells = jnp.concatenate(
            [
                lax.ppermute(tail, axis, [(i, (i + 1) % count) for i in range(ends)]),
                cells,
                lax.ppermute(head, axis, [((i + 1) % count, i) for i in range(ends)]),
            ],
            axis=dim,
        )
    return cells


def band_matrix(kernel, length):
    extent = kernel.shape[0]
    row_index = jnp.arange(length, dtype=jnp.int32)[:, None]
    col_index = jnp.arange(length + extent - 1, dtype=jnp.int32)[None, :]
    offset = col_index - row_index
    choose = (offset[:, :, None] == jnp.arange(extent, dtype=jnp.int32)[None, None, :]).astype(
        jnp.float32
    )
    return jnp.sum(choose * kernel[None, None, :], axis=2)


def lateral_matrix(kernel, displacement, length):
    extent = kernel.shape[0]
    radius = (extent - 1) // 2
    row_index = jnp.arange(length, dtype=jnp.int32)[:, None]
    col_index = jnp.arange(length, dtype=jnp.int32)[None, :]
    offset = col_index - row_index + radius + displacement
    choose = (offset[:, :, None] == jnp.arange(extent, dtype=jnp.int32)[None, None, :]).astype(
        jnp.float32
    )
    return jnp.sum(choose * kernel[None, None, :], axis=2)


def normalize(kernel):
    return kernel / jnp.sum(kernel, axis=-1, keepdims=True)


def blur_forward(haloed, band_depth, band_rows, lateral):
    section = jnp.einsum("zj,jyx->zyx", band_depth, haloed, precision=exact_mode)
    section = jnp.einsum("yj,zjx->zyx", band_rows, section, precision=exact_mode)
    return jnp.einsum("zyj,xj->zyx", section, lateral, precision=exact_mode)


def local(
    prior_estimate,
    views_upright,
    views_turned,
    kernel_depth,
    kernel_rows,
    kernel_columns,
    lateral_offsets,
    block_views,
):
    depth, rows, columns = prior_estimate.shape
    count_views = kernel_depth.shape[0]
    count_blocks = block_views.shape[0]
    count_active = block_views.shape[1]
    reach_depth = (kernel_depth.shape[1] - 1) // 2
    reach_rows = (kernel_rows.shape[1] - 1) // 2
    turned = jnp.transpose(
        lax.all_to_all(views_turned, "xy", split_axis=3, concat_axis=2, tiled=True), (0, 1, 3, 2)
    )
    observed = jnp.concatenate([views_upright, turned], axis=0)
    taps_depth = normalize(kernel_depth)
    taps_rows = normalize(kernel_rows)
    taps_columns = normalize(kernel_columns)
    forward_depth = [band_matrix(taps_depth[number], depth) for number in range(count_views)]
    forward_rows = [band_matrix(taps_rows[number], rows) for number in range(count_views)]
    laterals = [
        lateral_matrix(taps_columns[number], lateral_offsets[number], columns)
        for number in range(count_views)
    ]
    member = (
        jnp.sum(
            (
                block_views[:, :, None] == jnp.arange(count_views, dtype=jnp.int32)[None, None, :]
            ).astype(jnp.float32),
            axis=1,
        )
        / count_active
    )
    side_count = lax.axis_size("xy")
    here_depth = lax.axis_index("gz")
    here_rows = lax.axis_index("xy")
    block_list = jnp.arange(count_blocks, dtype=jnp.int32)
    own_id = here_depth * side_count + here_rows
    picker = (block_list == own_id).astype(jnp.float32)
    own_weights = jnp.dot(picker, member, precision=exact_mode)
    adjoint_depth = [band_matrix(taps_depth[number][::-1], depth) for number in range(count_views)]
    adjoint_rows = [band_matrix(taps_rows[number][::-1], rows) for number in range(count_views)]
    estimate = prior_estimate
    for iteration in range(ITERS):
        haloed = padded(estimate, (("xy", 1),), reach_rows)
        haloed = padded(haloed, (("gz", 0),), reach_depth)
        correction = jnp.zeros_like(estimate)
        for number in range(count_views):
            blurred = blur_forward(
                haloed, forward_depth[number], forward_rows[number], laterals[number]
            )
            quotient = observed[number] / blurred
            rimmed = padded(quotient, (("xy", 1),), reach_rows)
            rimmed = padded(rimmed, (("gz", 0),), reach_depth)
            back = jnp.einsum("zj,jyx->zyx", adjoint_depth[number], rimmed, precision=exact_mode)
            back = jnp.einsum("yj,zjx->zyx", adjoint_rows[number], back, precision=exact_mode)
            back = jnp.einsum("zyj,jx->zyx", back, laterals[number], precision=exact_mode)
            correction = correction + own_weights[number] * back
        estimate = estimate * correction
    return estimate


def solution(mesh):
    in_specs = (
        P("gz", "xy", None),
        P(None, "gz", "xy", None),
        P(None, "gz", "xy", None),
        P(),
        P(),
        P(),
        P(),
        P(),
    )
    out_specs = P("gz", "xy", None)
    return jax.shard_map(local, mesh=mesh, in_specs=in_specs, out_specs=out_specs, check_vma=False)
```

profile of v0, /device:TPU:31, one launch (start us, length us, event | category | flops | bytes accessed | tf_op | source)
XLA Modules:
  0.0 543.5 jit_solution(17599730964510681161)
XLA Ops:
  7.6 5.5 %copy.134 = f32[3,48,16,256]{1,2,0,3:T(8,128)} copy(f32[3,48,16,256]{3,2,1,0:T(8,128)S(1)} %copy-done.8) | data formatting | bytes 4718592 | tf_op args[2]
  13.1 9.5 %reshape.154 = f32[8,1,73728]{2,1,0:T(1,128)} reshape(f32[256,3,16,48]{3,2,1,0:T(8,128)} %bitcast.336) | data formatting | bytes 4718592
  22.6 6.2 %all-to-all-start = ((f32[8,1,73728]{2,1,0:T(1,128)}), f32[8,1,73728]{2,1,0:T(1,128)S(1)}, u32[]{:S(2)}, u32[]{:S(2)}) async-start(f32[8,1,73728]{2,1,0:T(1,128)} %reshape.154), calls=%async_computation | async-start | bytes 4718592 | tf_op jit(solution)/shard_map/all_to_all | solution.py:77
  69.8 5.6 %collective-permute-start.2 = (f32[30,62,128]{2,1,0:T(8,128)S(1)}, f32[30,62,128]{2,1,0:T(8,128)S(1)}, u32[]{:S(2)}, u32[]{:S(2)}) collective-permute-start(f32[30,62,128]{2,1,0:T(8,128)S(1)} %copy.121), channel_id=1, source_target_pairs={{0,8},{8,16},{16,24},{24,32},{32,40},{40,48},{48,56},{56,64},{64,7... | collective-permute-start | bytes 2856968 | tf_op jit(solution)/shard_map/ppermute | solution.py:18
  124.8 5.5 %collective-permute-start.8 = (f32[48,15,128]{2,1,0:T(8,128)S(1)}, f32[48,15,128]{2,1,0:T(8,128)S(1)}, u32[]{:S(2)}, u32[]{:S(2)}) collective-permute-start(f32[48,15,128]{2,1,0:T(8,128)S(1)} %get-tuple-element.73), channel_id=1, source_target_pairs={{0,1},{1,2},{2,3},{3,4},{4,5},{5,6},{6,7},{8,9},{9,10},{10,11},{11... | collective-permute-start | bytes 1105928 | tf_op jit(solution)/shard_map/ppermute | solution.py:18
  139.2 8.2 %collective-permute-done.4 = f32[48,15,128]{2,1,0:T(8,128)S(1)} collective-permute-done((f32[48,15,128]{2,1,0:T(8,128)S(1)}, f32[48,15,128]{2,1,0:T(8,128)S(1)}, u32[]{:S(2)}, u32[]{:S(2)}) %collective-permute-start.4) | collective-permute-done | bytes 368672 | tf_op jit(solution)/shard_map/ppermute | solution.py:18
  152.3 8.7 %reduce = f32[8,73728]{1,0:T(8,128)} reduce(f32[8,1,73728]{2,1,0:T(1,128)S(1)} %all-to-all-done, f32[]{:T(128)} %broadcast.179), dimensions={1}, to_apply=%all_to_all.13.reduce_sub_computation | reduce | bytes 4718596 | tf_op jit(solution)/shard_map/all_to_all | solution.py:77
  161.1 6.8 %reshape.155 = f32[256,3,16,48]{3,2,1,0:T(8,128)} reshape(f32[8,73728]{1,0:T(8,128)} %reduce) | data formatting | bytes 4718592
  167.9 8.1 %copy.136 = f32[3,48,8,16,32]{1,4,3,2,0:T(8,128)} copy(f32[3,48,8,16,32]{1,3,0,4,2:T(8,128)} %bitcast.334) | data formatting | bytes 4718592 | tf_op jit(solution)/shard_map/all_to_all | solution.py:77
  175.9 5.9 %copy.137 = f32[3,48,128,32]{2,3,1,0:T(8,128)S(1)} copy(f32[3,48,128,32]{1,3,2,0:T(8,128)} %bitcast.335) | data formatting | bytes 4718592 | tf_op jit(solution)/shard_map/all_to_all | solution.py:77
  185.9 6.2 %collective-permute-start.24 = (f32[48,15,128]{2,1,0:T(8,128)S(1)}, f32[48,15,128]{2,1,0:T(8,128)S(1)}, u32[]{:S(2)}, u32[]{:S(2)}) collective-permute-start(f32[48,15,128]{2,1,0:T(8,128)S(1)} %get-tuple-element.81), channel_id=1, source_target_pairs={{0,1},{1,2},{2,3},{3,4},{4,5},{5,6},{6,7},{8,9},{9,10},{10,11},{11... | collective-permute-start | bytes 1105928 | tf_op jit(solution)/shard_map/ppermute | solution.py:18
  194.9 5.5 %collective-permute-start.20 = (f32[48,15,128]{2,1,0:T(8,128)S(1)}, f32[48,15,128]{2,1,0:T(8,128)S(1)}, u32[]{:S(2)}, u32[]{:S(2)}) collective-permute-start(f32[48,15,128]{2,1,0:T(8,128)S(1)} %get-tuple-element.79), channel_id=1, source_target_pairs={{0,1},{1,2},{2,3},{3,4},{4,5},{5,6},{6,7},{8,9},{9,10},{10,11},{11... | collective-permute-start | bytes 1105928 | tf_op jit(solution)/shard_map/ppermute | solution.py:18
  203.4 5.5 %collective-permute-start.16 = (f32[48,15,128]{2,1,0:T(8,128)S(1)}, f32[48,15,128]{2,1,0:T(8,128)S(1)}, u32[]{:S(2)}, u32[]{:S(2)}) collective-permute-start(f32[48,15,128]{2,1,0:T(8,128)S(1)} %get-tuple-element.77), channel_id=1, source_target_pairs={{0,1},{1,2},{2,3},{3,4},{4,5},{5,6},{6,7},{8,9},{9,10},{10,11},{11... | collective-permute-start | bytes 1105928 | tf_op jit(solution)/shard_map/ppermute | solution.py:18
  221.0 7.3 %collective-permute-start.10 = (f32[30,62,128]{2,1,0:T(8,128)S(1)}, f32[30,62,128]{2,1,0:T(8,128)S(1)}, u32[]{:S(2)}, u32[]{:S(2)}) collective-permute-start(f32[30,62,128]{2,1,0:T(8,128)S(1)} %copy-done.19), channel_id=1, source_target_pairs={{0,8},{8,16},{16,24},{24,32},{32,40},{40,48},{48,56},{56,64},{64,7... | collective-permute-start | bytes 2856968 | tf_op jit(solution)/shard_map/ppermute | solution.py:18
  231.1 7.4 %collective-permute-start.6 = (f32[30,62,128]{2,1,0:T(8,128)S(1)}, f32[30,62,128]{2,1,0:T(8,128)S(1)}, u32[]{:S(2)}, u32[]{:S(2)}) collective-permute-start(f32[30,62,128]{2,1,0:T(8,128)S(1)} %get-tuple-element.43), channel_id=1, source_target_pairs={{0,8},{8,16},{16,24},{24,32},{32,40},{40,48},{48,56},{56,64},{64,7... | collective-permute-start | bytes 2856968 | tf_op jit(solution)/shard_map/ppermute | solution.py:18
  247.0 7.3 %collective-permute-start.26 = (f32[30,62,128]{2,1,0:T(8,128)S(1)}, f32[30,62,128]{2,1,0:T(8,128)S(1)}, u32[]{:S(2)}, u32[]{:S(2)}) collective-permute-start(f32[30,62,128]{2,1,0:T(8,128)S(1)} %get-tuple-element.53), channel_id=1, source_target_pairs={{0,8},{8,16},{16,24},{24,32},{32,40},{40,48},{48,56},{56,64},{64,7... | collective-permute-start | bytes 2856968 | tf_op jit(solution)/shard_map/ppermute | solution.py:18
  264.4 7.3 %collective-permute-start.22 = (f32[30,62,128]{2,1,0:T(8,128)S(1)}, f32[30,62,128]{2,1,0:T(8,128)S(1)}, u32[]{:S(2)}, u32[]{:S(2)}) collective-permute-start(f32[30,62,128]{2,1,0:T(8,128)S(1)} %get-tuple-element.51), channel_id=1, source_target_pairs={{0,8},{8,16},{16,24},{24,32},{32,40},{40,48},{48,56},{56,64},{64,7... | collective-permute-start | bytes 2856968 | tf_op jit(solution)/shard_map/ppermute | solution.py:18
  281.6 7.5 %collective-permute-start.18 = (f32[30,62,128]{2,1,0:T(8,128)S(1)}, f32[30,62,128]{2,1,0:T(8,128)S(1)}, u32[]{:S(2)}, u32[]{:S(2)}) collective-permute-start(f32[30,62,128]{2,1,0:T(8,128)S(1)} %get-tuple-element.49), channel_id=1, source_target_pairs={{0,8},{8,16},{16,24},{24,32},{32,40},{40,48},{48,56},{56,64},{64,7... | collective-permute-start | bytes 2856968 | tf_op jit(solution)/shard_map/ppermute | solution.py:18
  316.1 5.5 %collective-permute-start.28 = (f32[48,15,128]{2,1,0:T(8,128)S(1)}, f32[48,15,128]{2,1,0:T(8,128)S(1)}, u32[]{:S(2)}, u32[]{:S(2)}) collective-permute-start(f32[48,15,128]{2,1,0:T(8,128)S(1)} %get-tuple-element.69), channel_id=1, source_target_pairs={{0,1},{1,2},{2,3},{3,4},{4,5},{5,6},{6,7},{8,9},{9,10},{10,11},{11... | collective-permute-start | bytes 1105928 | tf_op jit(solution)/shard_map/ppermute | solution.py:18
  328.7 7.4 %collective-permute-start.30 = (f32[30,62,128]{2,1,0:T(8,128)S(1)}, f32[30,62,128]{2,1,0:T(8,128)S(1)}, u32[]{:S(2)}, u32[]{:S(2)}) collective-permute-start(f32[30,62,128]{2,1,0:T(8,128)S(1)} %get-tuple-element.41), channel_id=1, source_target_pairs={{0,8},{8,16},{16,24},{24,32},{32,40},{40,48},{48,56},{56,64},{64,7... | collective-permute-start | bytes 2856968 | tf_op jit(solution)/shard_map/ppermute | solution.py:18
  336.1 9.7 %collective-permute-done.31 = f32[30,62,128]{2,1,0:T(8,128)S(1)} collective-permute-done((f32[30,62,128]{2,1,0:T(8,128)S(1)}, f32[30,62,128]{2,1,0:T(8,128)S(1)}, u32[]{:S(2)}, u32[]{:S(2)}) %collective-permute-start.31) | collective-permute-done | bytes 952352 | tf_op jit(solution)/shard_map/ppermute | solution.py:20
  376.7 5.9 %collective-permute-start.52 = (f32[48,15,128]{2,1,0:T(8,128)S(1)}, f32[48,15,128]{2,1,0:T(8,128)S(1)}, u32[]{:S(2)}, u32[]{:S(2)}) collective-permute-start(f32[48,15,128]{2,1,0:T(8,128)S(1)} %get-tuple-element.67), channel_id=1, source_target_pairs={{0,1},{1,2},{2,3},{3,4},{4,5},{5,6},{6,7},{8,9},{9,10},{10,11},{11... | collective-permute-start | bytes 1105928 | tf_op jit(solution)/shard_map/ppermute | solution.py:18
  386.9 5.5 %collective-permute-start.48 = (f32[48,15,128]{2,1,0:T(8,128)S(1)}, f32[48,15,128]{2,1,0:T(8,128)S(1)}, u32[]{:S(2)}, u32[]{:S(2)}) collective-permute-start(f32[48,15,128]{2,1,0:T(8,128)S(1)} %get-tuple-element.65), channel_id=1, source_target_pairs={{0,1},{1,2},{2,3},{3,4},{4,5},{5,6},{6,7},{8,9},{9,10},{10,11},{11... | collective-permute-start | bytes 1105928 | tf_op jit(solution)/shard_map/ppermute | solution.py:18
  404.3 5.5 %collective-permute-start.44 = (f32[48,15,128]{2,1,0:T(8,128)S(1)}, f32[48,15,128]{2,1,0:T(8,128)S(1)}, u32[]{:S(2)}, u32[]{:S(2)}) collective-permute-start(f32[48,15,128]{2,1,0:T(8,128)S(1)} %get-tuple-element.63), channel_id=1, source_target_pairs={{0,1},{1,2},{2,3},{3,4},{4,5},{5,6},{6,7},{8,9},{9,10},{10,11},{11... | collective-permute-start | bytes 1105928 | tf_op jit(solution)/shard_map/ppermute | solution.py:18
  412.0 5.5 %collective-permute-start.40 = (f32[48,15,128]{2,1,0:T(8,128)S(1)}, f32[48,15,128]{2,1,0:T(8,128)S(1)}, u32[]{:S(2)}, u32[]{:S(2)}) collective-permute-start(f32[48,15,128]{2,1,0:T(8,128)S(1)} %get-tuple-element.61), channel_id=1, source_target_pairs={{0,1},{1,2},{2,3},{3,4},{4,5},{5,6},{6,7},{8,9},{9,10},{10,11},{11... | collective-permute-start | bytes 1105928 | tf_op jit(solution)/shard_map/ppermute | solution.py:18
  419.7 5.5 %collective-permute-start.36 = (f32[48,15,128]{2,1,0:T(8,128)S(1)}, f32[48,15,128]{2,1,0:T(8,128)S(1)}, u32[]{:S(2)}, u32[]{:S(2)}) collective-permute-start(f32[48,15,128]{2,1,0:T(8,128)S(1)} %get-tuple-element.59), channel_id=1, source_target_pairs={{0,1},{1,2},{2,3},{3,4},{4,5},{5,6},{6,7},{8,9},{9,10},{10,11},{11... | collective-permute-start | bytes 1105928 | tf_op jit(solution)/shard_map/ppermute | solution.py:18
  435.4 11.7 %collective-permute-start.54 = (f32[30,62,128]{2,1,0:T(8,128)S(1)}, f32[30,62,128]{2,1,0:T(8,128)S(1)}, u32[]{:S(2)}, u32[]{:S(2)}) collective-permute-start(f32[30,62,128]{2,1,0:T(8,128)S(1)} %get-tuple-element.39), channel_id=1, source_target_pairs={{0,8},{8,16},{16,24},{24,32},{32,40},{40,48},{48,56},{56,64},{64,7... | collective-permute-start | bytes 2856968 | tf_op jit(solution)/shard_map/ppermute | solution.py:18
  449.5 7.3 %collective-permute-start.50 = (f32[30,62,128]{2,1,0:T(8,128)S(1)}, f32[30,62,128]{2,1,0:T(8,128)S(1)}, u32[]{:S(2)}, u32[]{:S(2)}) collective-permute-start(f32[30,62,128]{2,1,0:T(8,128)S(1)} %get-tuple-element.37), channel_id=1, source_target_pairs={{0,8},{8,16},{16,24},{24,32},{32,40},{40,48},{48,56},{56,64},{64,7... | collective-permute-start | bytes 2856968 | tf_op jit(solution)/shard_map/ppermute | solution.py:18
  459.5 7.3 %collective-permute-start.46 = (f32[30,62,128]{2,1,0:T(8,128)S(1)}, f32[30,62,128]{2,1,0:T(8,128)S(1)}, u32[]{:S(2)}, u32[]{:S(2)}) collective-permute-start(f32[30,62,128]{2,1,0:T(8,128)S(1)} %get-tuple-element.35), channel_id=1, source_target_pairs={{0,8},{8,16},{16,24},{24,32},{32,40},{40,48},{48,56},{56,64},{64,7... | collective-permute-start | bytes 2856968 | tf_op jit(solution)/shard_map/ppermute | solution.py:18
  477.3 7.3 %collective-permute-start.42 = (f32[30,62,128]{2,1,0:T(8,128)S(1)}, f32[30,62,128]{2,1,0:T(8,128)S(1)}, u32[]{:S(2)}, u32[]{:S(2)}) collective-permute-start(f32[30,62,128]{2,1,0:T(8,128)S(1)} %get-tuple-element.33), channel_id=1, source_target_pairs={{0,8},{8,16},{16,24},{24,32},{32,40},{40,48},{48,56},{56,64},{64,7... | collective-permute-start | bytes 2856968 | tf_op jit(solution)/shard_map/ppermute | solution.py:18
  494.4 7.3 %collective-permute-start.38 = (f32[30,62,128]{2,1,0:T(8,128)S(1)}, f32[30,62,128]{2,1,0:T(8,128)S(1)}, u32[]{:S(2)}, u32[]{:S(2)}) collective-permute-start(f32[30,62,128]{2,1,0:T(8,128)S(1)} %get-tuple-element.31), channel_id=1, source_target_pairs={{0,8},{8,16},{16,24},{24,32},{32,40},{40,48},{48,56},{56,64},{64,7... | collective-permute-start | bytes 2856968 | tf_op jit(solution)/shard_map/ppermute | solution.py:18
  511.6 7.4 %collective-permute-start.34 = (f32[30,62,128]{2,1,0:T(8,128)S(1)}, f32[30,62,128]{2,1,0:T(8,128)S(1)}, u32[]{:S(2)}, u32[]{:S(2)}) collective-permute-start(f32[30,62,128]{2,1,0:T(8,128)S(1)} %get-tuple-element.29), channel_id=1, source_target_pairs={{0,8},{8,16},{16,24},{24,32},{32,40},{40,48},{48,56},{56,64},{64,7... | collective-permute-start | bytes 2856968 | tf_op jit(solution)/shard_map/ppermute | solution.py:18
  (502 shorter events, 317.7 us)
Async XLA Ops:
  2.2 59.6 %collective-permute-start = (f32[48,15,128]{2,0,1:T(8,128)}, f32[48,15,128]{2,0,1:T(8,128)}, u32[]{:S(2)}, u32[]{:S(2)}) collective-permute-start(f32[48,15,128]{2,0,1:T(8,128)} %copy.306), channel_id=1, source_target_pairs={{0,1},{1,2},{2,3},{3,4},{4,5},{5,6},{6,7},{8,9},{9,10},{10,11},{11... | collective-permute-start | bytes 1105928 | tf_op jit(solution)/shard_map/ppermute | solution.py:18
  5.5 57.8 %collective-permute-start.1 = (f32[48,15,128]{2,0,1:T(8,128)S(1)}, f32[48,15,128]{2,0,1:T(8,128)}, u32[]{:S(2)}, u32[]{:S(2)}) collective-permute-start(f32[48,15,128]{2,0,1:T(8,128)S(1)} %copy.307), channel_id=1, source_target_pairs={{1,0},{2,1},{3,2},{4,3},{5,4},{6,5},{7,6},{9,8},{10,9},{11,10},{12... | collective-permute-start | bytes 1105928 | tf_op jit(solution)/shard_map/ppermute | solution.py:20
  22.6 129.2 %all-to-all-start = ((f32[8,1,73728]{2,1,0:T(1,128)}), f32[8,1,73728]{2,1,0:T(1,128)S(1)}, u32[]{:S(2)}, u32[]{:S(2)}) async-start(f32[8,1,73728]{2,1,0:T(1,128)} %reshape.154), calls=%async_computation | async-start | bytes 4718592 | tf_op jit(solution)/shard_map/all_to_all | solution.py:77
  94.0 36.3 %collective-permute-start.13 = (f32[48,15,128]{2,1,0:T(8,128)S(1)}, f32[48,15,128]{2,1,0:T(8,128)S(1)}, u32[]{:S(2)}, u32[]{:S(2)}) collective-permute-start(f32[48,15,128]{2,1,0:T(8,128)S(1)} %get-tuple-element.76), channel_id=1, source_target_pairs={{1,0},{2,1},{3,2},{4,3},{5,4},{6,5},{7,6},{9,8},{10,9},{11,10},{12... | collective-permute-start | bytes 1105928 | tf_op jit(solution)/shard_map/ppermute | solution.py:20
  96.5 39.8 %collective-permute-start.12 = (f32[48,15,128]{2,1,0:T(8,128)S(1)}, f32[48,15,128]{2,1,0:T(8,128)S(1)}, u32[]{:S(2)}, u32[]{:S(2)}) collective-permute-start(f32[48,15,128]{2,1,0:T(8,128)S(1)} %get-tuple-element.75), channel_id=1, source_target_pairs={{0,1},{1,2},{2,3},{3,4},{4,5},{5,6},{6,7},{8,9},{9,10},{10,11},{11... | collective-permute-start | bytes 1105928 | tf_op jit(solution)/shard_map/ppermute | solution.py:18
  106.3 30.1 %collective-permute-start.9 = (f32[48,15,128]{2,1,0:T(8,128)S(1)}, f32[48,15,128]{2,1,0:T(8,128)S(1)}, u32[]{:S(2)}, u32[]{:S(2)}) collective-permute-start(f32[48,15,128]{2,1,0:T(8,128)S(1)} %get-tuple-element.74), channel_id=1, source_target_pairs={{1,0},{2,1},{3,2},{4,3},{5,4},{6,5},{7,6},{9,8},{10,9},{11,10},{12... | collective-permute-start | bytes 1105928 | tf_op jit(solution)/shard_map/ppermute | solution.py:20
  218.9 28.1 %collective-permute-start.11 = (f32[30,62,128]{2,1,0:T(8,128)S(1)}, f32[30,62,128]{2,1,0:T(8,128)S(1)}, u32[]{:S(2)}, u32[]{:S(2)}) collective-permute-start(f32[30,62,128]{2,1,0:T(8,128)S(1)} %copy-done.20), channel_id=1, source_target_pairs={{8,0},{16,8},{24,16},{32,24},{40,32},{48,40},{56,48},{64,56},{72,6... | collective-permute-start | bytes 2856968 | tf_op jit(solution)/shard_map/ppermute | solution.py:20
  221.0 33.2 %collective-permute-start.10 = (f32[30,62,128]{2,1,0:T(8,128)S(1)}, f32[30,62,128]{2,1,0:T(8,128)S(1)}, u32[]{:S(2)}, u32[]{:S(2)}) collective-permute-start(f32[30,62,128]{2,1,0:T(8,128)S(1)} %copy-done.19), channel_id=1, source_target_pairs={{0,8},{8,16},{16,24},{24,32},{32,40},{40,48},{48,56},{56,64},{64,7... | collective-permute-start | bytes 2856968 | tf_op jit(solution)/shard_map/ppermute | solution.py:18
  228.3 36.1 %collective-permute-start.7 = (f32[30,62,128]{2,1,0:T(8,128)S(1)}, f32[30,62,128]{2,1,0:T(8,128)S(1)}, u32[]{:S(2)}, u32[]{:S(2)}) collective-permute-start(f32[30,62,128]{2,1,0:T(8,128)S(1)} %get-tuple-element.44), channel_id=1, source_target_pairs={{8,0},{16,8},{24,16},{32,24},{40,32},{48,40},{56,48},{64,56},{72,6... | collective-permute-start | bytes 2856968 | tf_op jit(solution)/shard_map/ppermute | solution.py:20
  231.1 40.5 %collective-permute-start.6 = (f32[30,62,128]{2,1,0:T(8,128)S(1)}, f32[30,62,128]{2,1,0:T(8,128)S(1)}, u32[]{:S(2)}, u32[]{:S(2)}) collective-permute-start(f32[30,62,128]{2,1,0:T(8,128)S(1)} %get-tuple-element.43), channel_id=1, source_target_pairs={{0,8},{8,16},{16,24},{24,32},{32,40},{40,48},{48,56},{56,64},{64,7... | collective-permute-start | bytes 2856968 | tf_op jit(solution)/shard_map/ppermute | solution.py:18
  238.6 43.0 %collective-permute-start.27 = (f32[30,62,128]{2,1,0:T(8,128)S(1)}, f32[30,62,128]{2,1,0:T(8,128)S(1)}, u32[]{:S(2)}, u32[]{:S(2)}) collective-permute-start(f32[30,62,128]{2,1,0:T(8,128)S(1)} %get-tuple-element.54), channel_id=1, source_target_pairs={{8,0},{16,8},{24,16},{32,24},{40,32},{48,40},{56,48},{64,56},{72,6... | collective-permute-start | bytes 2856968 | tf_op jit(solution)/shard_map/ppermute | solution.py:20
  247.0 42.1 %collective-permute-start.26 = (f32[30,62,128]{2,1,0:T(8,128)S(1)}, f32[30,62,128]{2,1,0:T(8,128)S(1)}, u32[]{:S(2)}, u32[]{:S(2)}) collective-permute-start(f32[30,62,128]{2,1,0:T(8,128)S(1)} %get-tuple-element.53), channel_id=1, source_target_pairs={{0,8},{8,16},{16,24},{24,32},{32,40},{40,48},{48,56},{56,64},{64,7... | collective-permute-start | bytes 2856968 | tf_op jit(solution)/shard_map/ppermute | solution.py:18
  254.3 42.5 %collective-permute-start.23 = (f32[30,62,128]{2,1,0:T(8,128)S(1)}, f32[30,62,128]{2,1,0:T(8,128)S(1)}, u32[]{:S(2)}, u32[]{:S(2)}) collective-permute-start(f32[30,62,128]{2,1,0:T(8,128)S(1)} %get-tuple-element.52), channel_id=1, source_target_pairs={{8,0},{16,8},{24,16},{32,24},{40,32},{48,40},{56,48},{64,56},{72,6... | collective-permute-start | bytes 2856968 | tf_op jit(solution)/shard_map/ppermute | solution.py:20
  264.4 32.3 %collective-permute-start.22 = (f32[30,62,128]{2,1,0:T(8,128)S(1)}, f32[30,62,128]{2,1,0:T(8,128)S(1)}, u32[]{:S(2)}, u32[]{:S(2)}) collective-permute-start(f32[30,62,128]{2,1,0:T(8,128)S(1)} %get-tuple-element.51), channel_id=1, source_target_pairs={{0,8},{8,16},{16,24},{24,32},{32,40},{40,48},{48,56},{56,64},{64,7... | collective-permute-start | bytes 2856968 | tf_op jit(solution)/shard_map/ppermute | solution.py:18
  271.7 33.1 %collective-permute-start.19 = (f32[30,62,128]{2,1,0:T(8,128)S(1)}, f32[30,62,128]{2,1,0:T(8,128)S(1)}, u32[]{:S(2)}, u32[]{:S(2)}) collective-permute-start(f32[30,62,128]{2,1,0:T(8,128)S(1)} %get-tuple-element.50), channel_id=1, source_target_pairs={{8,0},{16,8},{24,16},{32,24},{40,32},{48,40},{56,48},{64,56},{72,6... | collective-permute-start | bytes 2856968 | tf_op jit(solution)/shard_map/ppermute | solution.py:20
  374.7 29.6 %collective-permute-start.53 = (f32[48,15,128]{2,1,0:T(8,128)S(1)}, f32[48,15,128]{2,1,0:T(8,128)S(1)}, u32[]{:S(2)}, u32[]{:S(2)}) collective-permute-start(f32[48,15,128]{2,1,0:T(8,128)S(1)} %get-tuple-element.68), channel_id=1, source_target_pairs={{1,0},{2,1},{3,2},{4,3},{5,4},{6,5},{7,6},{9,8},{10,9},{11,10},{12... | collective-permute-start | bytes 1105928 | tf_op jit(solution)/shard_map/ppermute | solution.py:20
  376.7 33.2 %collective-permute-start.52 = (f32[48,15,128]{2,1,0:T(8,128)S(1)}, f32[48,15,128]{2,1,0:T(8,128)S(1)}, u32[]{:S(2)}, u32[]{:S(2)}) collective-permute-start(f32[48,15,128]{2,1,0:T(8,128)S(1)} %get-tuple-element.67), channel_id=1, source_target_pairs={{0,1},{1,2},{2,3},{3,4},{4,5},{5,6},{6,7},{8,9},{9,10},{10,11},{11... | collective-permute-start | bytes 1105928 | tf_op jit(solution)/shard_map/ppermute | solution.py:18
  385.0 27.0 %collective-permute-start.49 = (f32[48,15,128]{2,1,0:T(8,128)S(1)}, f32[48,15,128]{2,1,0:T(8,128)S(1)}, u32[]{:S(2)}, u32[]{:S(2)}) collective-permute-start(f32[48,15,128]{2,1,0:T(8,128)S(1)} %get-tuple-element.66), channel_id=1, source_target_pairs={{1,0},{2,1},{3,2},{4,3},{5,4},{6,5},{7,6},{9,8},{10,9},{11,10},{12... | collective-permute-start | bytes 1105928 | tf_op jit(solution)/shard_map/ppermute | solution.py:20
  386.9 30.6 %collective-permute-start.48 = (f32[48,15,128]{2,1,0:T(8,128)S(1)}, f32[48,15,128]{2,1,0:T(8,128)S(1)}, u32[]{:S(2)}, u32[]{:S(2)}) collective-permute-start(f32[48,15,128]{2,1,0:T(8,128)S(1)} %get-tuple-element.65), channel_id=1, source_target_pairs={{0,1},{1,2},{2,3},{3,4},{4,5},{5,6},{6,7},{8,9},{9,10},{10,11},{11... | collective-permute-start | bytes 1105928 | tf_op jit(solution)/shard_map/ppermute | solution.py:18
  419.7 27.4 %collective-permute-start.36 = (f32[48,15,128]{2,1,0:T(8,128)S(1)}, f32[48,15,128]{2,1,0:T(8,128)S(1)}, u32[]{:S(2)}, u32[]{:S(2)}) collective-permute-start(f32[48,15,128]{2,1,0:T(8,128)S(1)} %get-tuple-element.59), channel_id=1, source_target_pairs={{0,1},{1,2},{2,3},{3,4},{4,5},{5,6},{6,7},{8,9},{9,10},{10,11},{11... | collective-permute-start | bytes 1105928 | tf_op jit(solution)/shard_map/ppermute | solution.py:18
  427.5 29.2 %collective-permute-start.32 = (f32[48,15,128]{2,1,0:T(8,128)S(1)}, f32[48,15,128]{2,1,0:T(8,128)S(1)}, u32[]{:S(2)}, u32[]{:S(2)}) collective-permute-start(f32[48,15,128]{2,1,0:T(8,128)S(1)} %get-tuple-element.57), channel_id=1, source_target_pairs={{0,1},{1,2},{2,3},{3,4},{4,5},{5,6},{6,7},{8,9},{9,10},{10,11},{11... | collective-permute-start | bytes 1105928 | tf_op jit(solution)/shard_map/ppermute | solution.py:18
  433.0 26.5 %collective-permute-start.55 = (f32[30,62,128]{2,1,0:T(8,128)S(1)}, f32[30,62,128]{2,1,0:T(8,128)S(1)}, u32[]{:S(2)}, u32[]{:S(2)}) collective-permute-start(f32[30,62,128]{2,1,0:T(8,128)S(1)} %get-tuple-element.40), channel_id=1, source_target_pairs={{8,0},{16,8},{24,16},{32,24},{40,32},{48,40},{56,48},{64,56},{72,6... | collective-permute-start | bytes 2856968 | tf_op jit(solution)/shard_map/ppermute | solution.py:20
  435.4 31.4 %collective-permute-start.54 = (f32[30,62,128]{2,1,0:T(8,128)S(1)}, f32[30,62,128]{2,1,0:T(8,128)S(1)}, u32[]{:S(2)}, u32[]{:S(2)}) collective-permute-start(f32[30,62,128]{2,1,0:T(8,128)S(1)} %get-tuple-element.39), channel_id=1, source_target_pairs={{0,8},{8,16},{16,24},{24,32},{32,40},{40,48},{48,56},{56,64},{64,7... | collective-permute-start | bytes 2856968 | tf_op jit(solution)/shard_map/ppermute | solution.py:18
  447.1 30.2 %collective-permute-start.51 = (f32[30,62,128]{2,1,0:T(8,128)S(1)}, f32[30,62,128]{2,1,0:T(8,128)S(1)}, u32[]{:S(2)}, u32[]{:S(2)}) collective-permute-start(f32[30,62,128]{2,1,0:T(8,128)S(1)} %get-tuple-element.38), channel_id=1, source_target_pairs={{8,0},{16,8},{24,16},{32,24},{40,32},{48,40},{56,48},{64,56},{72,6... | collective-permute-start | bytes 2856968 | tf_op jit(solution)/shard_map/ppermute | solution.py:20
  449.5 35.2 %collective-permute-start.50 = (f32[30,62,128]{2,1,0:T(8,128)S(1)}, f32[30,62,128]{2,1,0:T(8,128)S(1)}, u32[]{:S(2)}, u32[]{:S(2)}) collective-permute-start(f32[30,62,128]{2,1,0:T(8,128)S(1)} %get-tuple-element.37), channel_id=1, source_target_pairs={{0,8},{8,16},{16,24},{24,32},{32,40},{40,48},{48,56},{56,64},{64,7... | collective-permute-start | bytes 2856968 | tf_op jit(solution)/shard_map/ppermute | solution.py:18
  456.7 37.6 %collective-permute-start.47 = (f32[30,62,128]{2,1,0:T(8,128)S(1)}, f32[30,62,128]{2,1,0:T(8,128)S(1)}, u32[]{:S(2)}, u32[]{:S(2)}) collective-permute-start(f32[30,62,128]{2,1,0:T(8,128)S(1)} %get-tuple-element.36), channel_id=1, source_target_pairs={{8,0},{16,8},{24,16},{32,24},{40,32},{48,40},{56,48},{64,56},{72,6... | collective-permute-start | bytes 2856968 | tf_op jit(solution)/shard_map/ppermute | solution.py:20
  459.5 42.1 %collective-permute-start.46 = (f32[30,62,128]{2,1,0:T(8,128)S(1)}, f32[30,62,128]{2,1,0:T(8,128)S(1)}, u32[]{:S(2)}, u32[]{:S(2)}) collective-permute-start(f32[30,62,128]{2,1,0:T(8,128)S(1)} %get-tuple-element.35), channel_id=1, source_target_pairs={{0,8},{8,16},{16,24},{24,32},{32,40},{40,48},{48,56},{56,64},{64,7... | collective-permute-start | bytes 2856968 | tf_op jit(solution)/shard_map/ppermute | solution.py:18
  466.8 44.7 %collective-permute-start.43 = (f32[30,62,128]{2,1,0:T(8,128)S(1)}, f32[30,62,128]{2,1,0:T(8,128)S(1)}, u32[]{:S(2)}, u32[]{:S(2)}) collective-permute-start(f32[30,62,128]{2,1,0:T(8,128)S(1)} %get-tuple-element.34), channel_id=1, source_target_pairs={{8,0},{16,8},{24,16},{32,24},{40,32},{48,40},{56,48},{64,56},{72,6... | collective-permute-start | bytes 2856968 | tf_op jit(solution)/shard_map/ppermute | solution.py:20
  477.3 41.7 %collective-permute-start.42 = (f32[30,62,128]{2,1,0:T(8,128)S(1)}, f32[30,62,128]{2,1,0:T(8,128)S(1)}, u32[]{:S(2)}, u32[]{:S(2)}) collective-permute-start(f32[30,62,128]{2,1,0:T(8,128)S(1)} %get-tuple-element.33), channel_id=1, source_target_pairs={{0,8},{8,16},{16,24},{24,32},{32,40},{40,48},{48,56},{56,64},{64,7... | collective-permute-start | bytes 2856968 | tf_op jit(solution)/shard_map/ppermute | solution.py:18
  484.6 42.0 %collective-permute-start.39 = (f32[30,62,128]{2,1,0:T(8,128)S(1)}, f32[30,62,128]{2,1,0:T(8,128)S(1)}, u32[]{:S(2)}, u32[]{:S(2)}) collective-permute-start(f32[30,62,128]{2,1,0:T(8,128)S(1)} %get-tuple-element.32), channel_id=1, source_target_pairs={{8,0},{16,8},{24,16},{32,24},{40,32},{48,40},{56,48},{64,56},{72,6... | collective-permute-start | bytes 2856968 | tf_op jit(solution)/shard_map/ppermute | solution.py:20
  494.4 32.2 %collective-permute-start.38 = (f32[30,62,128]{2,1,0:T(8,128)S(1)}, f32[30,62,128]{2,1,0:T(8,128)S(1)}, u32[]{:S(2)}, u32[]{:S(2)}) collective-permute-start(f32[30,62,128]{2,1,0:T(8,128)S(1)} %get-tuple-element.31), channel_id=1, source_target_pairs={{0,8},{8,16},{16,24},{24,32},{32,40},{40,48},{48,56},{56,64},{64,7... | collective-permute-start | bytes 2856968 | tf_op jit(solution)/shard_map/ppermute | solution.py:18
  501.7 32.9 %collective-permute-start.35 = (f32[30,62,128]{2,1,0:T(8,128)S(1)}, f32[30,62,128]{2,1,0:T(8,128)S(1)}, u32[]{:S(2)}, u32[]{:S(2)}) collective-permute-start(f32[30,62,128]{2,1,0:T(8,128)S(1)} %get-tuple-element.30), channel_id=1, source_target_pairs={{8,0},{16,8},{24,16},{32,24},{40,32},{48,40},{56,48},{64,56},{72,6... | collective-permute-start | bytes 2856968 | tf_op jit(solution)/shard_map/ppermute | solution.py:20
  (145 other events, 2070.2 us)
where the time goes:
time: 552 us; the launch traced here: 544 us
  starting transfers between devices  244 us (44%)
  matrix products  156 us (28%)
  local copies, waits for them, and re-layouts  68.4 us (12%)
  other arithmetic  41.3 us (7%)
  waiting for transfers between devices  30.5 us (6%)
    ppermute x28, starting transfers between devices, padded(): lax.ppermute(tail, axis, [(i, (i + 1) % count) for i in range(ends)])  176 us
    ppermute x28, starting transfers between devices, padded(): lax.ppermute(head, axis, [((i + 1) % count, i) for i in range(ends)])  61.3 us
    dot_general x12, matrix products, local(): jnp.einsum('zj,jyx->zyx', adjoint_depth[number], rimmed, precision=exact_...  48.6 us
    dot_general x12, matrix products, blur_forward(): jnp.einsum('zj,jyx->zyx', band_depth, haloed, precision=exact_mode)  37.9 us
    unnamed x247, local copies, waits for them, and re-layouts  25.3 us
    dot_general x12, matrix products, blur_forward(): jnp.einsum('yj,zjx->zyx', band_rows, section, precision=exact_mode)  21.3 us
    dot_general x12, matrix products, local(): jnp.einsum('yj,zjx->zyx', adjoint_rows[number], back, precision=exact_mode)  18.9 us
    dot_general x12, matrix products, local(): jnp.einsum('zyj,jx->zyx', back, laterals[number], precision=exact_mode)  18.1 us
  transfers between devices with their start and end apart: 57, of which 8 were waited for; matrix products, arithmetic and copies ran while one was open for 34% of the time, Pallas kernels for 0%

commit v1 on v0

--- a/solution.py
+++ b/solution.py
@@ -5,6 +5,13 @@
 
 ITERS = 2
 exact_mode = lax.Precision.HIGHEST
+
+
+def exchange_blocks(x, axis, split, join):
+    devices = lax.axis_size(axis)
+    parts = jnp.stack(jnp.split(x, devices, axis=split), axis=0)
+    parts = lax.all_to_all(parts, axis, split_axis=0, concat_axis=0)
+    return jnp.concatenate(parts, axis=join)
 
 
 def padded(cells, sides, width):
@@ -73,9 +80,7 @@
     count_active = block_views.shape[1]
     reach_depth = (kernel_depth.shape[1] - 1) // 2
     reach_rows = (kernel_rows.shape[1] - 1) // 2
-    turned = jnp.transpose(
-        lax.all_to_all(views_turned, "xy", split_axis=3, concat_axis=2, tiled=True), (0, 1, 3, 2)
-    )
+    turned = jnp.transpose(exchange_blocks(views_turned, "xy", 3, 2), (0, 1, 3, 2))
     observed = jnp.concatenate([views_upright, turned], axis=0)
     taps_depth = normalize(kernel_depth)
     taps_rows = normalize(kernel_rows)

time: 552 us -> 559 us (1.013)
  the two profiles are of different devices: /device:TPU:31 before, /device:TPU:104 now
where the time goes in v1:
time: 559 us; the launch traced here: 548 us
  starting transfers between devices  217 us (39%)
  matrix products  156 us (28%)
  local copies, waits for them, and re-layouts  79.5 us (14%)
  waiting for transfers between devices  59.6 us (11%)
  other arithmetic  33.1 us (6%)
    ppermute x28, starting transfers between devices, padded(): lax.ppermute(head, axis, [((i + 1) % count, i) for i in range(ends)])  147 us
    ppermute x28, starting transfers between devices, padded(): lax.ppermute(tail, axis, [(i, (i + 1) % count) for i in range(ends)])  63.5 us
    dot_general x12, matrix products, local(): jnp.einsum('zj,jyx->zyx', adjoint_depth[number], rimmed, precision=exact_...  48.7 us
    ppermute x28, waiting for transfers between devices, padded(): lax.ppermute(tail, axis, [(i, (i + 1) % count) for i in range(ends)])  45.3 us
    unnamed x243, local copies, waits for them, and re-layouts  42.7 us
    dot_general x12, matrix products, blur_forward(): jnp.einsum('zj,jyx->zyx', band_depth, haloed, precision=exact_mode)  37.8 us
    dot_general x12, matrix products, blur_forward(): jnp.einsum('yj,zjx->zyx', band_rows, section, precision=exact_mode)  21.3 us
    dot_general x12, matrix products, local(): jnp.einsum('yj,zjx->zyx', adjoint_rows[number], back, precision=exact_mode)  18.9 us
  transfers between devices with their start and end apart: 57, of which 12 were waited for; matrix products, arithmetic and copies ran while one was open for 33% of the time, Pallas kernels for 0%

profile of v1, /device:TPU:104, one launch (start us, length us, event | category | flops | bytes accessed | tf_op | source)
XLA Modules:
  0.0 547.9 jit_solution(10288373198801928763)
XLA Ops:
  8.9 4.4 fusion.259
  36.4 9.5 %reshape.162 = f32[8,1,73728]{2,1,0:T(1,128)} reshape(f32[8,3,16,32,48]{4,3,2,1,0:T(8,128)} %bitcast.321) | data formatting | bytes 4718592
  45.9 6.5 %all-to-all-start = ((f32[8,1,73728]{2,1,0:T(1,128)}), f32[8,1,73728]{2,1,0:T(1,128)S(1)}, u32[]{:S(2)}, u32[]{:S(2)}) async-start(f32[8,1,73728]{2,1,0:T(1,128)} %reshape.162), calls=%async_computation | async-start | bytes 4718592 | tf_op jit(solution)/shard_map/all_to_all | solution.py:13
  80.7 8.0 %collective-permute-done.3 = f32[30,62,128]{2,1,0:T(8,128)S(1)} collective-permute-done((f32[30,62,128]{2,1,0:T(8,128)S(1)}, f32[30,62,128]{2,1,0:T(8,128)S(1)}, u32[]{:S(2)}, u32[]{:S(2)}) %collective-permute-start.3) | collective-permute-done | bytes 952352 | tf_op jit(solution)/shard_map/ppermute | solution.py:27
  133.3 5.4 collective-permute-start.13
  149.1 8.7 %reduce = f32[8,73728]{1,0:T(8,128)} reduce(f32[8,1,73728]{2,1,0:T(1,128)S(1)} %all-to-all-done, f32[]{:T(128)} %broadcast.179), dimensions={1}, to_apply=%all_to_all.3.reduce_sub_computation | reduce | bytes 4718596 | tf_op jit(solution)/shard_map/all_to_all | solution.py:13
  157.8 6.8 %reshape.163 = f32[8,3,16,32,48]{4,3,2,1,0:T(8,128)} reshape(f32[8,73728]{1,0:T(8,128)} %reduce) | data formatting | bytes 4718592
  171.6 5.9 %copy.155 = f32[3,48,128,32]{2,3,1,0:T(8,128)S(1)} copy(f32[3,48,128,32]{1,3,2,0:T(8,128)} %bitcast.349) | data formatting | bytes 4718592 | tf_op jit(solution)/shard_map/reshape | solution.py:14
  188.7 6.0 %collective-permute-start.25 = (f32[48,15,128]{2,1,0:T(8,128)S(1)}, f32[48,15,128]{2,1,0:T(8,128)S(1)}, u32[]{:S(2)}, u32[]{:S(2)}) collective-permute-start(f32[48,15,128]{2,1,0:T(8,128)S(1)} %get-tuple-element.90), channel_id=1, source_target_pairs={{1,0},{2,1},{3,2},{4,3},{5,4},{6,5},{7,6},{9,8},{10,9},{11,10},{12... | collective-permute-start | bytes 1105928 | tf_op jit(solution)/shard_map/ppermute | solution.py:27
  197.8 4.4 collective-permute-done.24
  202.2 5.7 %collective-permute-start.21 = (f32[48,15,128]{2,1,0:T(8,128)S(1)}, f32[48,15,128]{2,1,0:T(8,128)S(1)}, u32[]{:S(2)}, u32[]{:S(2)}) collective-permute-start(f32[48,15,128]{2,1,0:T(8,128)S(1)} %get-tuple-element.88), channel_id=1, source_target_pairs={{1,0},{2,1},{3,2},{4,3},{5,4},{6,5},{7,6},{9,8},{10,9},{11,10},{12... | collective-permute-start | bytes 1105928 | tf_op jit(solution)/shard_map/ppermute | solution.py:27
  213.8 7.3 %collective-permute-start.15 = (f32[30,62,128]{2,1,0:T(8,128)S(1)}, f32[30,62,128]{2,1,0:T(8,128)S(1)}, u32[]{:S(2)}, u32[]{:S(2)}) collective-permute-start(f32[30,62,128]{2,1,0:T(8,128)S(1)} %copy-done.27), channel_id=1, source_target_pairs={{8,0},{16,8},{24,16},{32,24},{40,32},{48,40},{56,48},{64,56},{72,6... | collective-permute-start | bytes 2856968 | tf_op jit(solution)/shard_map/ppermute | solution.py:27
  223.2 7.3 %collective-permute-start.11 = (f32[30,62,128]{2,1,0:T(8,128)}, f32[30,62,128]{2,1,0:T(8,128)S(1)}, u32[]{:S(2)}, u32[]{:S(2)}) collective-permute-start(f32[30,62,128]{2,1,0:T(8,128)} %get-tuple-element.54), channel_id=1, source_target_pairs={{8,0},{16,8},{24,16},{32,24},{40,32},{48,40},{56,48},{64,56},{72,6... | collective-permute-start | bytes 2856968 | tf_op jit(solution)/shard_map/ppermute | solution.py:27
  231.4 7.9 %collective-permute-done.14 = f32[30,62,128]{2,1,0:T(8,128)S(1)} collective-permute-done((f32[30,62,128]{2,1,0:T(8,128)S(1)}, f32[30,62,128]{2,1,0:T(8,128)S(1)}, u32[]{:S(2)}, u32[]{:S(2)}) %collective-permute-start.14) | collective-permute-done | bytes 952352 | tf_op jit(solution)/shard_map/ppermute | solution.py:25
  250.1 6.8 %collective-permute-start.27 = (f32[30,62,128]{2,1,0:T(8,128)S(1)}, f32[30,62,128]{2,1,0:T(8,128)S(1)}, u32[]{:S(2)}, u32[]{:S(2)}) collective-permute-start(f32[30,62,128]{2,1,0:T(8,128)S(1)} %get-tuple-element.62), channel_id=1, source_target_pairs={{8,0},{16,8},{24,16},{32,24},{40,32},{48,40},{56,48},{64,56},{72,6... | collective-permute-start | bytes 2856968 | tf_op jit(solution)/shard_map/ppermute | solution.py:27
  267.0 7.3 %collective-permute-start.23 = (f32[30,62,128]{2,1,0:T(8,128)S(1)}, f32[30,62,128]{2,1,0:T(8,128)S(1)}, u32[]{:S(2)}, u32[]{:S(2)}) collective-permute-start(f32[30,62,128]{2,1,0:T(8,128)S(1)} %get-tuple-element.60), channel_id=1, source_target_pairs={{8,0},{16,8},{24,16},{32,24},{40,32},{48,40},{56,48},{64,56},{72,6... | collective-permute-start | bytes 2856968 | tf_op jit(solution)/shard_map/ppermute | solution.py:27
  284.2 7.5 %collective-permute-start.19 = (f32[30,62,128]{2,1,0:T(8,128)S(1)}, f32[30,62,128]{2,1,0:T(8,128)S(1)}, u32[]{:S(2)}, u32[]{:S(2)}) collective-permute-start(f32[30,62,128]{2,1,0:T(8,128)S(1)} %get-tuple-element.58), channel_id=1, source_target_pairs={{8,0},{16,8},{24,16},{32,24},{40,32},{48,40},{56,48},{64,56},{72,6... | collective-permute-start | bytes 2856968 | tf_op jit(solution)/shard_map/ppermute | solution.py:27
  330.6 7.4 %collective-permute-start.31 = (f32[30,62,128]{2,1,0:T(8,128)S(1)}, f32[30,62,128]{2,1,0:T(8,128)S(1)}, u32[]{:S(2)}, u32[]{:S(2)}) collective-permute-start(f32[30,62,128]{2,1,0:T(8,128)S(1)} %get-tuple-element.50), channel_id=1, source_target_pairs={{8,0},{16,8},{24,16},{32,24},{40,32},{48,40},{56,48},{64,56},{72,6... | collective-permute-start | bytes 2856968 | tf_op jit(solution)/shard_map/ppermute | solution.py:27
  338.0 9.7 %collective-permute-done.30 = f32[30,62,128]{2,1,0:T(8,128)S(1)} collective-permute-done((f32[30,62,128]{2,1,0:T(8,128)S(1)}, f32[30,62,128]{2,1,0:T(8,128)S(1)}, u32[]{:S(2)}, u32[]{:S(2)}) %collective-permute-start.30) | collective-permute-done | bytes 952352 | tf_op jit(solution)/shard_map/ppermute | solution.py:25
  362.1 4.2 fusion.26
  386.4 4.1 collective-permute-start.49
  397.2 6.1 %collective-permute-start.53 = (f32[48,15,128]{2,1,0:T(8,128)S(1)}, f32[48,15,128]{2,1,0:T(8,128)S(1)}, u32[]{:S(2)}, u32[]{:S(2)}) collective-permute-start(f32[48,15,128]{2,1,0:T(8,128)S(1)} %get-tuple-element.76), channel_id=1, source_target_pairs={{1,0},{2,1},{3,2},{4,3},{5,4},{6,5},{7,6},{9,8},{10,9},{11,10},{12... | collective-permute-start | bytes 1105928 | tf_op jit(solution)/shard_map/ppermute | solution.py:27
  408.5 6.7 %collective-permute-start.33 = (f32[48,15,128]{2,1,0:T(8,128)S(1)}, f32[48,15,128]{2,1,0:T(8,128)S(1)}, u32[]{:S(2)}, u32[]{:S(2)}) collective-permute-start(f32[48,15,128]{2,1,0:T(8,128)S(1)} %get-tuple-element.66), channel_id=1, source_target_pairs={{1,0},{2,1},{3,2},{4,3},{5,4},{6,5},{7,6},{9,8},{10,9},{11,10},{12... | collective-permute-start | bytes 1105928 | tf_op jit(solution)/shard_map/ppermute | solution.py:27
  417.4 5.3 collective-permute-start.37
  431.1 8.1 %collective-permute-done.44 = f32[48,15,128]{2,1,0:T(8,128)S(1)} collective-permute-done((f32[48,15,128]{2,1,0:T(8,128)S(1)}, f32[48,15,128]{2,1,0:T(8,128)S(1)}, u32[]{:S(2)}, u32[]{:S(2)}) %collective-permute-start.44) | collective-permute-done | bytes 368672 | tf_op jit(solution)/shard_map/ppermute | solution.py:25
  439.2 5.7 %collective-permute-start.41 = (f32[48,15,128]{2,1,0:T(8,128)S(1)}, f32[48,15,128]{2,1,0:T(8,128)S(1)}, u32[]{:S(2)}, u32[]{:S(2)}) collective-permute-start(f32[48,15,128]{2,1,0:T(8,128)S(1)} %get-tuple-element.70), channel_id=1, source_target_pairs={{1,0},{2,1},{3,2},{4,3},{5,4},{6,5},{7,6},{9,8},{10,9},{11,10},{12... | collective-permute-start | bytes 1105928 | tf_op jit(solution)/shard_map/ppermute | solution.py:27
  447.3 7.3 %collective-permute-start.55 = (f32[30,62,128]{2,1,0:T(8,128)S(1)}, f32[30,62,128]{2,1,0:T(8,128)S(1)}, u32[]{:S(2)}, u32[]{:S(2)}) collective-permute-start(f32[30,62,128]{2,1,0:T(8,128)S(1)} %get-tuple-element.48), channel_id=1, source_target_pairs={{8,0},{16,8},{24,16},{32,24},{40,32},{48,40},{56,48},{64,56},{72,6... | collective-permute-start | bytes 2856968 | tf_op jit(solution)/shard_map/ppermute | solution.py:27
  458.9 7.3 %collective-permute-start.51 = (f32[30,62,128]{2,1,0:T(8,128)S(1)}, f32[30,62,128]{2,1,0:T(8,128)S(1)}, u32[]{:S(2)}, u32[]{:S(2)}) collective-permute-start(f32[30,62,128]{2,1,0:T(8,128)S(1)} %get-tuple-element.46), channel_id=1, source_target_pairs={{8,0},{16,8},{24,16},{32,24},{40,32},{48,40},{56,48},{64,56},{72,6... | collective-permute-start | bytes 2856968 | tf_op jit(solution)/shard_map/ppermute | solution.py:27
  472.2 4.8 fusion
  478.5 6.5 %collective-permute-done.50 = f32[30,62,128]{2,1,0:T(8,128)S(1)} collective-permute-done((f32[30,62,128]{2,1,0:T(8,128)S(1)}, f32[30,62,128]{2,1,0:T(8,128)S(1)}, u32[]{:S(2)}, u32[]{:S(2)}) %collective-permute-start.50) | collective-permute-done | bytes 952352 | tf_op jit(solution)/shard_map/ppermute | solution.py:25
  497.4 6.8 %collective-permute-start.43 = (f32[30,62,128]{2,1,0:T(8,128)S(1)}, f32[30,62,128]{2,1,0:T(8,128)S(1)}, u32[]{:S(2)}, u32[]{:S(2)}) collective-permute-start(f32[30,62,128]{2,1,0:T(8,128)S(1)} %get-tuple-element.42), channel_id=1, source_target_pairs={{8,0},{16,8},{24,16},{32,24},{40,32},{48,40},{56,48},{64,56},{72,6... | collective-permute-start | bytes 2856968 | tf_op jit(solution)/shard_map/ppermute | solution.py:27
  514.3 7.6 %collective-permute-start.39 = (f32[30,62,128]{2,1,0:T(8,128)S(1)}, f32[30,62,128]{2,1,0:T(8,128)S(1)}, u32[]{:S(2)}, u32[]{:S(2)}) collective-permute-start(f32[30,62,128]{2,1,0:T(8,128)S(1)} %get-tuple-element.40), channel_id=1, source_target_pairs={{8,0},{16,8},{24,16},{32,24},{40,32},{48,40},{56,48},{64,56},{72,6... | collective-permute-start | bytes 2856968 | tf_op jit(solution)/shard_map/ppermute | solution.py:27
  (501 shorter events, 331.7 us)
Async XLA Ops:
  2.2 62.7 %collective-permute-start = (f32[48,15,128]{2,0,1:T(8,128)}, f32[48,15,128]{2,0,1:T(8,128)}, u32[]{:S(2)}, u32[]{:S(2)}) collective-permute-start(f32[48,15,128]{2,0,1:T(8,128)} %copy.330), channel_id=1, source_target_pairs={{0,1},{1,2},{2,3},{3,4},{4,5},{5,6},{6,7},{8,9},{9,10},{10,11},{11... | collective-permute-start | bytes 1105928 | tf_op jit(solution)/shard_map/ppermute | solution.py:25
  6.5 59.8 %collective-permute-start.1 = (f32[48,15,128]{2,0,1:T(8,128)}, f32[48,15,128]{2,0,1:T(8,128)}, u32[]{:S(2)}, u32[]{:S(2)}) collective-permute-start(f32[48,15,128]{2,0,1:T(8,128)} %copy.331), channel_id=1, source_target_pairs={{1,0},{2,1},{3,2},{4,3},{5,4},{6,5},{7,6},{9,8},{10,9},{11,10},{12... | collective-permute-start | bytes 1105928 | tf_op jit(solution)/shard_map/ppermute | solution.py:27
  45.9 102.7 %all-to-all-start = ((f32[8,1,73728]{2,1,0:T(1,128)}), f32[8,1,73728]{2,1,0:T(1,128)S(1)}, u32[]{:S(2)}, u32[]{:S(2)}) async-start(f32[8,1,73728]{2,1,0:T(1,128)} %reshape.162), calls=%async_computation | async-start | bytes 4718592 | tf_op jit(solution)/shard_map/all_to_all | solution.py:13
  96.4 47.7 %collective-permute-start.8 = (f32[48,15,128]{2,1,0:T(8,128)S(1)}, f32[48,15,128]{2,1,0:T(8,128)S(1)}, u32[]{:S(2)}, u32[]{:S(2)}) collective-permute-start(f32[48,15,128]{2,1,0:T(8,128)S(1)} %get-tuple-element.81), channel_id=1, source_target_pairs={{0,1},{1,2},{2,3},{3,4},{4,5},{5,6},{6,7},{8,9},{9,10},{10,11},{11... | collective-permute-start | bytes 1105928 | tf_op jit(solution)/shard_map/ppermute | solution.py:25
  99.8 44.3 %collective-permute-start.9 = (f32[48,15,128]{2,1,0:T(8,128)S(1)}, f32[48,15,128]{2,1,0:T(8,128)S(1)}, u32[]{:S(2)}, u32[]{:S(2)}) collective-permute-start(f32[48,15,128]{2,1,0:T(8,128)S(1)} %get-tuple-element.82), channel_id=1, source_target_pairs={{1,0},{2,1},{3,2},{4,3},{5,4},{6,5},{7,6},{9,8},{10,9},{11,10},{12... | collective-permute-start | bytes 1105928 | tf_op jit(solution)/shard_map/ppermute | solution.py:27
  107.2 34.2 %collective-permute-start.12 = (f32[48,15,128]{2,1,0:T(8,128)S(1)}, f32[48,15,128]{2,1,0:T(8,128)S(1)}, u32[]{:S(2)}, u32[]{:S(2)}) collective-permute-start(f32[48,15,128]{2,1,0:T(8,128)S(1)} %get-tuple-element.83), channel_id=1, source_target_pairs={{0,1},{1,2},{2,3},{3,4},{4,5},{5,6},{6,7},{8,9},{9,10},{10,11},{11... | collective-permute-start | bytes 1105928 | tf_op jit(solution)/shard_map/ppermute | solution.py:25
  179.6 41.7 %collective-permute-start.16 = (f32[48,15,128]{2,1,0:T(8,128)S(1)}, f32[48,15,128]{2,1,0:T(8,128)S(1)}, u32[]{:S(2)}, u32[]{:S(2)}) collective-permute-start(f32[48,15,128]{2,1,0:T(8,128)S(1)} %get-tuple-element.85), channel_id=1, source_target_pairs={{0,1},{1,2},{2,3},{3,4},{4,5},{5,6},{6,7},{8,9},{9,10},{10,11},{11... | collective-permute-start | bytes 1105928 | tf_op jit(solution)/shard_map/ppermute | solution.py:25
  181.8 41.4 %collective-permute-start.17 = (f32[48,15,128]{2,1,0:T(8,128)S(1)}, f32[48,15,128]{2,1,0:T(8,128)S(1)}, u32[]{:S(2)}, u32[]{:S(2)}) collective-permute-start(f32[48,15,128]{2,1,0:T(8,128)S(1)} %get-tuple-element.86), channel_id=1, source_target_pairs={{1,0},{2,1},{3,2},{4,3},{5,4},{6,5},{7,6},{9,8},{10,9},{11,10},{12... | collective-permute-start | bytes 1105928 | tf_op jit(solution)/shard_map/ppermute | solution.py:27
  209.5 57.5 %collective-permute-start.6 = (f32[30,62,128]{2,1,0:T(8,128)S(1)}, f32[30,62,128]{2,1,0:T(8,128)S(1)}, u32[]{:S(2)}, u32[]{:S(2)}) collective-permute-start(f32[30,62,128]{2,1,0:T(8,128)S(1)} %copy-done.26), channel_id=1, source_target_pairs={{0,8},{8,16},{16,24},{24,32},{32,40},{40,48},{48,56},{56,64},{64,7... | collective-permute-start | bytes 2856968 | tf_op jit(solution)/shard_map/ppermute | solution.py:25
  211.8 27.4 %collective-permute-start.14 = (f32[30,62,128]{2,1,0:T(8,128)S(1)}, f32[30,62,128]{2,1,0:T(8,128)S(1)}, u32[]{:S(2)}, u32[]{:S(2)}) collective-permute-start(f32[30,62,128]{2,1,0:T(8,128)S(1)} %copy-done.28), channel_id=1, source_target_pairs={{0,8},{8,16},{16,24},{24,32},{32,40},{40,48},{48,56},{56,64},{64,7... | collective-permute-start | bytes 2856968 | tf_op jit(solution)/shard_map/ppermute | solution.py:25
  213.8 27.4 %collective-permute-start.15 = (f32[30,62,128]{2,1,0:T(8,128)S(1)}, f32[30,62,128]{2,1,0:T(8,128)S(1)}, u32[]{:S(2)}, u32[]{:S(2)}) collective-permute-start(f32[30,62,128]{2,1,0:T(8,128)S(1)} %copy-done.27), channel_id=1, source_target_pairs={{8,0},{16,8},{24,16},{32,24},{40,32},{48,40},{56,48},{64,56},{72,6... | collective-permute-start | bytes 2856968 | tf_op jit(solution)/shard_map/ppermute | solution.py:27
  221.3 28.8 %collective-permute-start.10 = (f32[30,62,128]{2,1,0:T(8,128)}, f32[30,62,128]{2,1,0:T(8,128)S(1)}, u32[]{:S(2)}, u32[]{:S(2)}) collective-permute-start(f32[30,62,128]{2,1,0:T(8,128)} %get-tuple-element.53), channel_id=1, source_target_pairs={{0,8},{8,16},{16,24},{24,32},{32,40},{40,48},{48,56},{56,64},{64,7... | collective-permute-start | bytes 2856968 | tf_op jit(solution)/shard_map/ppermute | solution.py:25
  223.2 33.6 %collective-permute-start.11 = (f32[30,62,128]{2,1,0:T(8,128)}, f32[30,62,128]{2,1,0:T(8,128)S(1)}, u32[]{:S(2)}, u32[]{:S(2)}) collective-permute-start(f32[30,62,128]{2,1,0:T(8,128)} %get-tuple-element.54), channel_id=1, source_target_pairs={{8,0},{16,8},{24,16},{32,24},{40,32},{48,40},{56,48},{64,56},{72,6... | collective-permute-start | bytes 2856968 | tf_op jit(solution)/shard_map/ppermute | solution.py:27
  239.2 35.0 %collective-permute-start.7 = (f32[30,62,128]{2,1,0:T(8,128)S(1)}, f32[30,62,128]{2,1,0:T(8,128)S(1)}, u32[]{:S(2)}, u32[]{:S(2)}) collective-permute-start(f32[30,62,128]{2,1,0:T(8,128)S(1)} %copy-done.25), channel_id=1, source_target_pairs={{8,0},{16,8},{24,16},{32,24},{40,32},{48,40},{56,48},{64,56},{72,6... | collective-permute-start | bytes 2856968 | tf_op jit(solution)/shard_map/ppermute | solution.py:27
  241.2 43.0 %collective-permute-start.26 = (f32[30,62,128]{2,1,0:T(8,128)S(1)}, f32[30,62,128]{2,1,0:T(8,128)S(1)}, u32[]{:S(2)}, u32[]{:S(2)}) collective-permute-start(f32[30,62,128]{2,1,0:T(8,128)S(1)} %get-tuple-element.61), channel_id=1, source_target_pairs={{0,8},{8,16},{16,24},{24,32},{32,40},{40,48},{48,56},{56,64},{64,7... | collective-permute-start | bytes 2856968 | tf_op jit(solution)/shard_map/ppermute | solution.py:25
  250.1 41.6 %collective-permute-start.27 = (f32[30,62,128]{2,1,0:T(8,128)S(1)}, f32[30,62,128]{2,1,0:T(8,128)S(1)}, u32[]{:S(2)}, u32[]{:S(2)}) collective-permute-start(f32[30,62,128]{2,1,0:T(8,128)S(1)} %get-tuple-element.62), channel_id=1, source_target_pairs={{8,0},{16,8},{24,16},{32,24},{40,32},{48,40},{56,48},{64,56},{72,6... | collective-permute-start | bytes 2856968 | tf_op jit(solution)/shard_map/ppermute | solution.py:27
  256.9 42.4 %collective-permute-start.22 = (f32[30,62,128]{2,1,0:T(8,128)S(1)}, f32[30,62,128]{2,1,0:T(8,128)S(1)}, u32[]{:S(2)}, u32[]{:S(2)}) collective-permute-start(f32[30,62,128]{2,1,0:T(8,128)S(1)} %get-tuple-element.59), channel_id=1, source_target_pairs={{0,8},{8,16},{16,24},{24,32},{32,40},{40,48},{48,56},{56,64},{64,7... | collective-permute-start | bytes 2856968 | tf_op jit(solution)/shard_map/ppermute | solution.py:25
  267.0 32.3 %collective-permute-start.23 = (f32[30,62,128]{2,1,0:T(8,128)S(1)}, f32[30,62,128]{2,1,0:T(8,128)S(1)}, u32[]{:S(2)}, u32[]{:S(2)}) collective-permute-start(f32[30,62,128]{2,1,0:T(8,128)S(1)} %get-tuple-element.60), channel_id=1, source_target_pairs={{8,0},{16,8},{24,16},{32,24},{40,32},{48,40},{56,48},{64,56},{72,6... | collective-permute-start | bytes 2856968 | tf_op jit(solution)/shard_map/ppermute | solution.py:27
  274.3 33.1 %collective-permute-start.18 = (f32[30,62,128]{2,1,0:T(8,128)S(1)}, f32[30,62,128]{2,1,0:T(8,128)S(1)}, u32[]{:S(2)}, u32[]{:S(2)}) collective-permute-start(f32[30,62,128]{2,1,0:T(8,128)S(1)} %get-tuple-element.57), channel_id=1, source_target_pairs={{0,8},{8,16},{16,24},{24,32},{32,40},{40,48},{48,56},{56,64},{64,7... | collective-permute-start | bytes 2856968 | tf_op jit(solution)/shard_map/ppermute | solution.py:25
  384.5 40.3 %collective-permute-start.48 = (f32[48,15,128]{2,1,0:T(8,128)S(1)}, f32[48,15,128]{2,1,0:T(8,128)S(1)}, u32[]{:S(2)}, u32[]{:S(2)}) collective-permute-start(f32[48,15,128]{2,1,0:T(8,128)S(1)} %get-tuple-element.73), channel_id=1, source_target_pairs={{0,1},{1,2},{2,3},{3,4},{4,5},{5,6},{6,7},{8,9},{9,10},{10,11},{11... | collective-permute-start | bytes 1105928 | tf_op jit(solution)/shard_map/ppermute | solution.py:25
  386.4 40.3 %collective-permute-start.49 = (f32[48,15,128]{2,1,0:T(8,128)S(1)}, f32[48,15,128]{2,1,0:T(8,128)S(1)}, u32[]{:S(2)}, u32[]{:S(2)}) collective-permute-start(f32[48,15,128]{2,1,0:T(8,128)S(1)} %get-tuple-element.74), channel_id=1, source_target_pairs={{1,0},{2,1},{3,2},{4,3},{5,4},{6,5},{7,6},{9,8},{10,9},{11,10},{12... | collective-permute-start | bytes 1105928 | tf_op jit(solution)/shard_map/ppermute | solution.py:27
  415.2 41.8 %collective-permute-start.36 = (f32[48,15,128]{2,1,0:T(8,128)S(1)}, f32[48,15,128]{2,1,0:T(8,128)S(1)}, u32[]{:S(2)}, u32[]{:S(2)}) collective-permute-start(f32[48,15,128]{2,1,0:T(8,128)S(1)} %get-tuple-element.67), channel_id=1, source_target_pairs={{0,1},{1,2},{2,3},{3,4},{4,5},{5,6},{6,7},{8,9},{9,10},{10,11},{11... | collective-permute-start | bytes 1105928 | tf_op jit(solution)/shard_map/ppermute | solution.py:25
  417.4 41.6 %collective-permute-start.37 = (f32[48,15,128]{2,1,0:T(8,128)S(1)}, f32[48,15,128]{2,1,0:T(8,128)S(1)}, u32[]{:S(2)}, u32[]{:S(2)}) collective-permute-start(f32[48,15,128]{2,1,0:T(8,128)S(1)} %get-tuple-element.68), channel_id=1, source_target_pairs={{1,0},{2,1},{3,2},{4,3},{5,4},{6,5},{7,6},{9,8},{10,9},{11,10},{12... | collective-permute-start | bytes 1105928 | tf_op jit(solution)/shard_map/ppermute | solution.py:27
  422.7 24.7 %collective-permute-start.40 = (f32[48,15,128]{2,1,0:T(8,128)S(1)}, f32[48,15,128]{2,1,0:T(8,128)S(1)}, u32[]{:S(2)}, u32[]{:S(2)}) collective-permute-start(f32[48,15,128]{2,1,0:T(8,128)S(1)} %get-tuple-element.69), channel_id=1, source_target_pairs={{0,1},{1,2},{2,3},{3,4},{4,5},{5,6},{6,7},{8,9},{9,10},{10,11},{11... | collective-permute-start | bytes 1105928 | tf_op jit(solution)/shard_map/ppermute | solution.py:25
  454.6 74.9 %collective-permute-start.34 = (f32[30,62,128]{2,1,0:T(8,128)S(1)}, f32[30,62,128]{2,1,0:T(8,128)S(1)}, u32[]{:S(2)}, u32[]{:S(2)}) collective-permute-start(f32[30,62,128]{2,1,0:T(8,128)S(1)} %get-tuple-element.37), channel_id=1, source_target_pairs={{0,8},{8,16},{16,24},{24,32},{32,40},{40,48},{48,56},{56,64},{64,7... | collective-permute-start | bytes 2856968 | tf_op jit(solution)/shard_map/ppermute | solution.py:25
  457.0 28.1 %collective-permute-start.50 = (f32[30,62,128]{2,1,0:T(8,128)S(1)}, f32[30,62,128]{2,1,0:T(8,128)S(1)}, u32[]{:S(2)}, u32[]{:S(2)}) collective-permute-start(f32[30,62,128]{2,1,0:T(8,128)S(1)} %get-tuple-element.45), channel_id=1, source_target_pairs={{0,8},{8,16},{16,24},{24,32},{32,40},{40,48},{48,56},{56,64},{64,7... | collective-permute-start | bytes 2856968 | tf_op jit(solution)/shard_map/ppermute | solution.py:25
  458.9 28.1 %collective-permute-start.51 = (f32[30,62,128]{2,1,0:T(8,128)S(1)}, f32[30,62,128]{2,1,0:T(8,128)S(1)}, u32[]{:S(2)}, u32[]{:S(2)}) collective-permute-start(f32[30,62,128]{2,1,0:T(8,128)S(1)} %get-tuple-element.46), channel_id=1, source_target_pairs={{8,0},{16,8},{24,16},{32,24},{40,32},{48,40},{56,48},{64,56},{72,6... | collective-permute-start | bytes 2856968 | tf_op jit(solution)/shard_map/ppermute | solution.py:27
  467.1 62.4 %collective-permute-start.35 = (f32[30,62,128]{2,1,0:T(8,128)S(1)}, f32[30,62,128]{2,1,0:T(8,128)S(1)}, u32[]{:S(2)}, u32[]{:S(2)}) collective-permute-start(f32[30,62,128]{2,1,0:T(8,128)S(1)} %get-tuple-element.38), channel_id=1, source_target_pairs={{8,0},{16,8},{24,16},{32,24},{40,32},{48,40},{56,48},{64,56},{72,6... | collective-permute-start | bytes 2856968 | tf_op jit(solution)/shard_map/ppermute | solution.py:27
  469.5 27.9 %collective-permute-start.46 = (f32[30,62,128]{2,1,0:T(8,128)S(1)}, f32[30,62,128]{2,1,0:T(8,128)S(1)}, u32[]{:S(2)}, u32[]{:S(2)}) collective-permute-start(f32[30,62,128]{2,1,0:T(8,128)S(1)} %get-tuple-element.43), channel_id=1, source_target_pairs={{0,8},{8,16},{16,24},{24,32},{32,40},{40,48},{48,56},{56,64},{64,7... | collective-permute-start | bytes 2856968 | tf_op jit(solution)/shard_map/ppermute | solution.py:25
  487.0 27.3 %collective-permute-start.42 = (f32[30,62,128]{2,1,0:T(8,128)S(1)}, f32[30,62,128]{2,1,0:T(8,128)S(1)}, u32[]{:S(2)}, u32[]{:S(2)}) collective-permute-start(f32[30,62,128]{2,1,0:T(8,128)S(1)} %get-tuple-element.41), channel_id=1, source_target_pairs={{0,8},{8,16},{16,24},{24,32},{32,40},{40,48},{48,56},{56,64},{64,7... | collective-permute-start | bytes 2856968 | tf_op jit(solution)/shard_map/ppermute | solution.py:25
  497.4 24.5 %collective-permute-start.43 = (f32[30,62,128]{2,1,0:T(8,128)S(1)}, f32[30,62,128]{2,1,0:T(8,128)S(1)}, u32[]{:S(2)}, u32[]{:S(2)}) collective-permute-start(f32[30,62,128]{2,1,0:T(8,128)S(1)} %get-tuple-element.42), channel_id=1, source_target_pairs={{8,0},{16,8},{24,16},{32,24},{40,32},{48,40},{56,48},{64,56},{72,6... | collective-permute-start | bytes 2856968 | tf_op jit(solution)/shard_map/ppermute | solution.py:27
  504.2 33.3 %collective-permute-start.38 = (f32[30,62,128]{2,1,0:T(8,128)S(1)}, f32[30,62,128]{2,1,0:T(8,128)S(1)}, u32[]{:S(2)}, u32[]{:S(2)}) collective-permute-start(f32[30,62,128]{2,1,0:T(8,128)S(1)} %get-tuple-element.39), channel_id=1, source_target_pairs={{0,8},{8,16},{16,24},{24,32},{32,40},{40,48},{48,56},{56,64},{64,7... | collective-permute-start | bytes 2856968 | tf_op jit(solution)/shard_map/ppermute | solution.py:25
  (136 other events, 1804.1 us)
